TPU v7x, 32 devices: a whole 2x2x4 slice. The times are simulated.
32 devices in a mesh: slab: 8 (over z, x), freq: 4 (over y, core).
Axes of the slice: x: 2, y: 2, z: 4, core: 2. Of those that a mesh axis runs over, the one named last changes fastest.
Arguments:
- partials: bfloat16 [8, 3, 2, 32, 32, 5, 256], P('slab', None, None, 'freq'), may hold values from -400 to 400
- rec_plane: int32 [8, 3, 2], P('slab'), may hold values from 0 to 1
- rec_count: int32 [8, 3], P('slab'), may hold values from 0 to 2, as said below
- rec_weight: bfloat16 [8, 3, 2, 256], P('slab'), may hold values from 0.25 to 1
- qweight: float32 [16, 256], P('slab'), as said below
Outputs:
- spectra: bfloat16 [8, 32, 2, 16, 5, 256], P('freq', None, None, 'slab')
- r_factor: float32 [8, 64, 64], P('freq')
Inputs may be any that keep to these rules, and one draw needn't show every extreme that they name: `rec_count`: at most 2 live records from one source to one destination, reached in every draw; a source's records to its own index number exactly 2; none leave the ends of the slab axis; some destination receives 2 from each of its three sources. `qweight`: positive.
All inputs are finite; a program needn't handle non-finite values.
Results may differ from a plain program's by a relative error of at most 0.0025.
The roundings to bfloat16 on the way count: a program that leaves them out, or rounds other values in their place, can miss the bound.
Values may be sent and summed in bfloat16 or wider, within the bound.
No kernel may reach another device: no remote copies, remote signals or barrier semaphores. Data moves between devices by JAX's collectives and lax.ppermute only.
A program may use at most 64 MiB of HBM per device.

v0:
```python
import math
import jax
import jax.numpy as jnp
from jax import lax
from jax.sharding import PartitionSpec as P

NT = 32
NY = 16
NZ = 16
NF = 8
TAPS = (-0.0625, 0.25, 0.625, 0.25, -0.0625)


def from_behind(value, axis, steps):
    count = lax.axis_size(axis)
    leading, last = (max(0, -steps), min(count, count - steps))
    return lax.ppermute(value, axis, [(source, source + steps) for source in range(leading, last)])


def padded_2(block, sides, width):
    for axis, dim in sides:
        count = lax.axis_size(axis)
        forward = [(i, i + 1) for i in range(count - 1)]
        backward = [(target, source) for source, target in forward]
        low = lax.ppermute(
            lax.slice_in_dim(block, block.shape[dim] - width, None, axis=dim), axis, forward
        )
        high = lax.ppermute(lax.slice_in_dim(block, 0, width, axis=dim), axis, backward)
        block = jnp.concatenate([low, block, high], axis=dim)
    return block


def band_matrix(size):
    index = jnp.arange(size)
    offset = index[None, :] - index[:, None]
    result = jnp.zeros((size, size), jnp.float32)
    for place in range(5):
        result = result + TAPS[place] * (offset == place - 2).astype(jnp.float32)
    return result


def dft_table():
    times = jnp.arange(NT).astype(jnp.float32)
    freqs = jnp.arange(NF).astype(jnp.float32) + 1.0
    window = 0.5 - 0.5 * jnp.cos(2.0 * math.pi * times / NT)
    factor = 1.0 / jnp.sqrt(jnp.sum(window * window))
    angle = 2.0 * math.pi * times[:, None] * freqs[None, :] / NT
    real_part = factor * window[:, None] * jnp.cos(angle)
    imag_part = -factor * window[:, None] * jnp.sin(angle)
    return jnp.stack([real_part, imag_part], axis=2)


def record_terms(pieces, weights, planes, counts, plane_total):
    slots = jnp.arange(pieces.shape[0])
    valid = slots < counts[0]
    select = ((planes[:, None] == jnp.arange(plane_total)[None, :]) & valid[:, None]).astype(
        jnp.float32
    )
    scaled = pieces.astype(jnp.float32) * weights.astype(jnp.float32)[:, None, None, None, :]
    return jnp.einsum("cq,cbtvp->qbtvp", select, scaled, precision=lax.Precision.HIGHEST)


def upper_factor(gram):
    return jnp.swapaxes(jnp.linalg.cholesky(gram), 1, 2)


def add_products(total, piece):
    return total + jnp.einsum("akij,akil->kjl", piece, piece, precision=lax.Precision.HIGHEST)


def body(partials, rec_plane, rec_count, rec_weight, qweight):
    plane_total = qweight.shape[0]
    points = qweight.shape[1]

    def side_terms(side):
        return record_terms(
            partials[0, side],
            rec_weight[0, side],
            rec_plane[0, side],
            rec_count[0, side : side + 1],
            plane_total,
        )

    total = side_terms(1)
    total = total + from_behind(side_terms(0), "slab", -1)
    total = total + from_behind(side_terms(2), "slab", 1)
    assembled = total.astype(jnp.bfloat16)
    padded = padded_2(assembled, (("slab", 0),), 2)
    kyz = jnp.kron(band_matrix(NY), band_matrix(NZ)).astype(jnp.bfloat16)
    across = jnp.dot(padded.reshape(-1, points), kyz, preferred_element_type=jnp.float32).reshape(
        padded.shape
    )
    smoothed = TAPS[0] * across[0:plane_total]
    for place in range(1, 5):
        smoothed = smoothed + TAPS[place] * across[place : place + plane_total]
    local_spec = jnp.einsum(
        "xbtvp,tkr->kbrxvp", smoothed, dft_table(), precision=lax.Precision.HIGHEST
    ).astype(jnp.bfloat16)
    spectra = lax.all_to_all(local_spec, "freq", split_axis=0, concat_axis=1, tiled=True)
    freq_count = spectra.shape[0]
    columns = 2 * spectra.shape[1]
    values = spectra.astype(jnp.float32).reshape(
        freq_count, columns, plane_total, spectra.shape[4], points
    )
    weighted = (values * qweight[None, None, :, None, :]).reshape(freq_count, columns, -1)
    flat_values = values.reshape(freq_count, columns, -1)
    gram = jnp.einsum("kcr,kdr->kcd", weighted, flat_values, precision=lax.Precision.HIGHEST)
    local_factor = upper_factor(gram)[None]
    empty = jnp.zeros(gram.shape, jnp.float32)
    summed = add_products(
        empty,
        lax.all_gather(local_factor.astype(jnp.bfloat16), "slab", axis=0, tiled=True).astype(
            jnp.float32
        ),
    )
    factor = upper_factor(summed)
    return (spectra, factor)


def solution(mesh):
    placed = (
        P("slab", None, None, "freq", None, None, None),
        P("slab", None, None),
        P("slab", None),
        P("slab", None, None, None),
        P("slab", None),
    )
    return jax.shard_map(
        body,
        mesh=mesh,
        in_specs=placed,
        out_specs=(P("freq", None, None, "slab", None, None), P("freq", None, None)),
        check_vma=False,
    )
```

profile of v0, /device:TPU:0, one launch (start us, length us, event | category | flops | bytes accessed | tf_op | source)
XLA Modules:
  0.0 303.7 jit_solution(14255040084964306091)
XLA Ops:
  1.3 1.4 fusion.54
  4.5 3.2 %convert_multiply_fusion.2 = (f32[2,8,32,5,256]{4,2,3,1,0:T(8,128)S(1)}, f32[2,8,32,5,256]{4,2,3,1,0:T(8,128)S(1)}, f32[2,8,32,5,256]{4,2,3,1,0:T(8,128)S(1)}) fusion(f32[2,256]{1,0:T(2,128)S(1)} %get-tuple-element.19, bf16[1,3,2,8,32,5,256]{6,4,5,3,2,1,0:T(8,128)(2,1)} %param.6, f32[2,256]{1,0:T(2,128)S(1)} %get-tuple-element.20, ...), kind=kLoop, calls=%fused_computation.12 | loop fusion | flops 3932160 | bytes 11802624 | tf_op jit(solution)/shard_map/mul | solution.py:59
  7.7 5.8 %fusion.9 = f32[2,8,32,5,256]{4,0,3,2,1:T(2,128)S(1)} fusion(f32[2,8,32,5,256]{4,2,3,1,0:T(8,128)S(1)} %get-tuple-element.18, pred[2]{0:T(512)(128)(4,1)S(1)} %iota_compare_fusion.3, s32[2]{0:T(128)S(1)} %get-tuple-element.15), kind=kOutput, calls=%fused_computation.19 | convolution fusion | flops 15728648 | bytes 5242890 | tf_op jit(solution)/shard_map/cq,cbtvp->qbtvp/dot_general | solution.py:60
  13.6 1.3 collective-permute-start
  15.5 5.8 %fusion.7 = f32[2,8,32,5,256]{4,0,3,2,1:T(2,128)S(1)} fusion(f32[2,8,32,5,256]{4,2,3,1,0:T(8,128)S(1)} %get-tuple-element.17, pred[2]{0:T(512)(128)(4,1)S(1)} %iota_compare_fusion.2, s32[2]{0:T(128)S(1)} %get-tuple-element.14), kind=kOutput, calls=%fused_computation.17 | convolution fusion | flops 15728648 | bytes 5242890 | tf_op jit(solution)/shard_map/cq,cbtvp->qbtvp/dot_general | solution.py:60
  21.4 5.7 %collective-permute-start.1 = (f32[2,8,32,5,256]{4,0,3,2,1:T(2,128)S(1)}, f32[2,8,32,5,256]{4,0,3,2,1:T(2,128)S(1)}, u32[]{:S(2)}, u32[]{:S(2)}) collective-permute-start(f32[2,8,32,5,256]{4,0,3,2,1:T(2,128)S(1)} %fusion.7), channel_id=1, source_target_pairs={{0,4},{4,8},{8,12},{12,16},{16,20},{20,24},{24,28},{1,5},{5,9},{9,... | collective-permute-start | bytes 7864328 | tf_op jit(solution)/shard_map/ppermute | solution.py:17
  27.7 47.6 %collective-permute-done = f32[2,8,32,5,256]{4,0,3,2,1:T(2,128)S(1)} collective-permute-done((f32[2,8,32,5,256]{4,0,3,2,1:T(2,128)S(1)}, f32[2,8,32,5,256]{4,0,3,2,1:T(2,128)S(1)}, u32[]{:S(2)}, u32[]{:S(2)}) %collective-permute-start) | collective-permute-done | bytes 2621472 | tf_op jit(solution)/shard_map/ppermute | solution.py:17
  75.3 56.3 %collective-permute-done.1 = f32[2,8,32,5,256]{4,0,3,2,1:T(2,128)S(1)} collective-permute-done((f32[2,8,32,5,256]{4,0,3,2,1:T(2,128)S(1)}, f32[2,8,32,5,256]{4,0,3,2,1:T(2,128)S(1)}, u32[]{:S(2)}, u32[]{:S(2)}) %collective-permute-start.1) | collective-permute-done | bytes 2621472 | tf_op jit(solution)/shard_map/ppermute | solution.py:17
  131.6 7.8 %add_convert_fusion = bf16[2,8,32,5,256]{4,0,3,2,1:T(2,128)(2,1)S(1)} fusion(f32[2,8,32,5,256]{4,0,3,2,1:T(2,128)S(1)} %collective-permute-done.1, f32[2,8,32,5,256]{4,0,3,2,1:T(2,128)S(1)} %collective-permute-done, f32[2,8,32,5,256]{4,2,3,1,0:T(8,128)S(1)} %get-tuple-element.16, pred[2]{0:T(512)(128)(4,1)S(1)} %iota_compare_fusion.4, ...), kind=kOutput, calls=%fused_computation.16 | convolution fusion | flops 17694728 | bytes 9175050 | tf_op jit(solution)/shard_map/cq,cbtvp->qbtvp/dot_general | solution.py:60
  139.4 5.5 %collective-permute-start.2 = (bf16[2,8,32,5,256]{4,0,3,2,1:T(2,128)(2,1)S(1)}, bf16[2,8,32,5,256]{4,0,3,2,1:T(2,128)(2,1)}, u32[]{:S(2)}, u32[]{:S(2)}) collective-permute-start(bf16[2,8,32,5,256]{4,0,3,2,1:T(2,128)(2,1)S(1)} %add_convert_fusion), channel_id=1, source_target_pairs={{0,4},{4,8},{8,12},{12,16},{16,20},{20,24},{24,28},{1,5},{5,9},{9,... | collective-permute-start | bytes 3932168 | tf_op jit(solution)/shard_map/ppermute | solution.py:25
  144.9 1.5 collective-permute-start.3
  149.2 50.9 %collective-permute-done.2 = bf16[2,8,32,5,256]{4,0,3,2,1:T(2,128)(2,1)} collective-permute-done((bf16[2,8,32,5,256]{4,0,3,2,1:T(2,128)(2,1)S(1)}, bf16[2,8,32,5,256]{4,0,3,2,1:T(2,128)(2,1)}, u32[]{:S(2)}, u32[]{:S(2)}) %collective-permute-start.2) | collective-permute-done | bytes 1310752 | tf_op jit(solution)/shard_map/ppermute | solution.py:25
  200.1 5.7 %pad_maximum_fusion = bf16[6,8,32,5,256]{4,0,3,2,1:T(8,128)(2,1)S(1)} fusion(bf16[2,8,32,5,256]{4,0,3,2,1:T(2,128)(2,1)} %collective-permute-done.3, bf16[2,8,32,5,256]{4,0,3,2,1:T(2,128)(2,1)S(1)} %add_convert_fusion, bf16[2,8,32,5,256]{4,0,3,2,1:T(2,128)(2,1)} %collective-permute-done.2), kind=kLoop, calls=%fused_computation | loop fusion | flops 11796480 | bytes 7864320 | tf_op jit(solution)/shard_map/concatenate | solution.py:29
  205.8 4.1 %copy.59 = bf16[6,8,32,5,256]{4,3,2,1,0:T(8,128)(2,1)} copy(bf16[6,8,32,5,256]{4,0,3,2,1:T(8,128)(2,1)S(1)} %pad_maximum_fusion) | data formatting | bytes 7864320 | tf_op jit(solution)/shard_map/concatenate | solution.py:29
  210.0 8.4 %reshape.309 = bf16[7680,256]{1,0:T(8,128)(2,1)} reshape(bf16[6,8,32,5,256]{4,3,2,1,0:T(8,128)(2,1)} %copy.59) | data formatting | bytes 7864320 | tf_op jit(solution)/shard_map/reshape | solution.py:90
  218.4 3.3 %fusion.55 = f32[7680,256]{1,0:T(8,128)S(1)} fusion(bf16[7680,256]{1,0:T(8,128)(2,1)} %reshape.309, bf16[256,256]{1,0:T(8,128)(2,1)S(1)} %convert_element_type.143), kind=kOutput, calls=%fused_computation.93 | convolution fusion | flops 1006632960 | bytes 11927552 | tf_op jit(solution)/shard_map/dot_general | solution.py:90
  222.5 2.1 reshape.316
  224.7 4.2 %fusion.21 = bf16[8,8,2,2,5,256]{5,0,4,1,3,2:T(8,128)(2,1)S(1)} fusion(f32[2,8,32,5,256]{4,3,2,1,0:T(8,128)} %reshape.316, f32[32,8,1]{0,1,2:T(8,128)S(1)} %get-tuple-element.23, f32[32,8,1]{0,1,2:T(8,128)S(1)} %get-tuple-element.22), kind=kOutput, calls=%fused_computation.28 | convolution fusion | flops 126157312 | bytes 3278848 | tf_op jit(solution)/shard_map/xbtvp,tkr->kbrxvp/dot_general | solution.py:96
  229.9 3.7 %all-to-all-start = ((bf16[8,8,2,2,5,256]{5,1,4,3,2,0:T(8,128)(2,1)}), bf16[8,8,2,2,5,256]{5,1,4,3,2,0:T(8,128)(2,1)S(1)}, u32[]{:S(2)}, u32[]{:S(2)}) async-start(bf16[8,8,2,2,5,256]{5,1,4,3,2,0:T(8,128)(2,1)} %copy.61), calls=%async_computation | async-start | bytes 1310720 | tf_op jit(solution)/shard_map/all_to_all | solution.py:99
  233.7 9.9 %all-to-all-done = bf16[8,8,2,2,5,256]{5,1,4,3,2,0:T(8,128)(2,1)S(1)} async-done(((bf16[8,8,2,2,5,256]{5,1,4,3,2,0:T(8,128)(2,1)}), bf16[8,8,2,2,5,256]{5,1,4,3,2,0:T(8,128)(2,1)S(1)}, u32[]{:S(2)}, u32[]{:S(2)}) %all-to-all-start) | async-done | bytes 655392 | tf_op jit(solution)/shard_map/all_to_all | solution.py:99
  245.4 11.7 %custom-call.4 = f32[2,64,64]{2,1,0:T(8,128)S(1)} custom-call(f32[2,64,64]{2,1,0:T(8,128)S(1)} %fusion.26), custom_call_target="Cholesky" | custom-call | tf_op jit(solution)/shard_map/jit(cholesky)/cholesky | solution.py:64
  257.5 31.8 %all-gather = bf16[16,64,64]{2,1,0:T(8,128)(2,1)S(1)} all-gather(bf16[2,64,64]{2,1,0:T(8,128)(2,1)S(1)} %copy.65), channel_id=2, replica_groups=mesh['slab'=8,'freq'=4] {'slab'}, dimensions={0}, use_global_device_ids=true | all-gather | bytes 147456 | tf_op jit(solution)/shard_map/all_gather | solution.py:112
  289.7 11.7 %custom-call.5 = f32[2,64,64]{2,1,0:T(8,128)S(1)} custom-call(f32[2,64,64]{2,1,0:T(8,128)S(1)} %fusion.25), custom_call_target="Cholesky" | custom-call | tf_op jit(solution)/shard_map/jit(cholesky)/cholesky | solution.py:64
  302.4 1.3 copy.63
  (38 shorter events, 11.1 us)
Async XLA Ops:
  13.6 61.7 %collective-permute-start = (f32[2,8,32,5,256]{4,0,3,2,1:T(2,128)S(1)}, f32[2,8,32,5,256]{4,0,3,2,1:T(2,128)S(1)}, u32[]{:S(2)}, u32[]{:S(2)}) collective-permute-start(f32[2,8,32,5,256]{4,0,3,2,1:T(2,128)S(1)} %fusion.9), channel_id=1, source_target_pairs={{4,0},{8,4},{12,8},{16,12},{20,16},{24,20},{28,24},{5,1},{9,5},{13... | collective-permute-start | bytes 7864328 | tf_op jit(solution)/shard_map/ppermute | solution.py:17
  21.4 110.3 %collective-permute-start.1 = (f32[2,8,32,5,256]{4,0,3,2,1:T(2,128)S(1)}, f32[2,8,32,5,256]{4,0,3,2,1:T(2,128)S(1)}, u32[]{:S(2)}, u32[]{:S(2)}) collective-permute-start(f32[2,8,32,5,256]{4,0,3,2,1:T(2,128)S(1)} %fusion.7), channel_id=1, source_target_pairs={{0,4},{4,8},{8,12},{12,16},{16,20},{20,24},{24,28},{1,5},{5,9},{9,... | collective-permute-start | bytes 7864328 | tf_op jit(solution)/shard_map/ppermute | solution.py:17
  139.4 60.7 %collective-permute-start.2 = (bf16[2,8,32,5,256]{4,0,3,2,1:T(2,128)(2,1)S(1)}, bf16[2,8,32,5,256]{4,0,3,2,1:T(2,128)(2,1)}, u32[]{:S(2)}, u32[]{:S(2)}) collective-permute-start(bf16[2,8,32,5,256]{4,0,3,2,1:T(2,128)(2,1)S(1)} %add_convert_fusion), channel_id=1, source_target_pairs={{0,4},{4,8},{8,12},{12,16},{16,20},{20,24},{24,28},{1,5},{5,9},{9,... | collective-permute-start | bytes 3932168 | tf_op jit(solution)/shard_map/ppermute | solution.py:25
  144.9 55.2 %collective-permute-start.3 = (bf16[2,8,32,5,256]{4,0,3,2,1:T(2,128)(2,1)S(1)}, bf16[2,8,32,5,256]{4,0,3,2,1:T(2,128)(2,1)}, u32[]{:S(2)}, u32[]{:S(2)}) collective-permute-start(bf16[2,8,32,5,256]{4,0,3,2,1:T(2,128)(2,1)S(1)} %add_convert_fusion), channel_id=1, source_target_pairs={{4,0},{8,4},{12,8},{16,12},{20,16},{24,20},{28,24},{5,1},{9,5},{13... | collective-permute-start | bytes 3932168 | tf_op jit(solution)/shard_map/ppermute | solution.py:28
  224.7 8.9 %copy-start = (f32[2,256]{1,0:T(2,128)S(1)}, f32[2,256]{1,0:T(2,128)}, u32[]{:S(2)}) copy-start(f32[2,256]{1,0:T(2,128)} %param.10) | copy-start | bytes 6148
  229.9 13.7 %all-to-all-start = ((bf16[8,8,2,2,5,256]{5,1,4,3,2,0:T(8,128)(2,1)}), bf16[8,8,2,2,5,256]{5,1,4,3,2,0:T(8,128)(2,1)S(1)}, u32[]{:S(2)}, u32[]{:S(2)}) async-start(bf16[8,8,2,2,5,256]{5,1,4,3,2,0:T(8,128)(2,1)} %copy.61), calls=%async_computation | async-start | bytes 1310720 | tf_op jit(solution)/shard_map/all_to_all | solution.py:99
where the time goes:
time: 304 us
  waiting for transfers between devices  165 us (54%)
  other arithmetic  37.6 us (12%)
  blocking collectives  31.8 us (10%)
  matrix products  28 us (9%)
  local copies, waits for them, and re-layouts  22.4 us (7%)
  starting transfers between devices  17.6 us (6%)
    ppermute x2, waiting for transfers between devices, from_behind(): lax.ppermute(value, axis, [(source, source + steps) for source in range(l...  104 us
    ppermute x1, waiting for transfers between devices, padded_2(): lax.ppermute(lax.slice_in_dim(block, block.shape[dim] - width, None, axis...  50.9 us
    all_gather x1, blocking collectives, body(): lax.all_gather(local_factor.astype(jnp.bfloat16), 'slab', axis=0, tiled=T...  31.8 us
    another operation x7, other arithmetic, upper_factor(): return jnp.swapaxes(jnp.linalg.cholesky(gram), 1, 2)  23.8 us
    dot_general x3, matrix products, record_terms(): jnp.einsum('cq,cbtvp->qbtvp', select, scaled, precision=lax.Precision.HIG...  19.4 us
    all_to_all x1, waiting for transfers between devices, body(): lax.all_to_all(local_spec, 'freq', split_axis=0, concat_axis=1, tiled=True)  9.9 us
    reshape x1, local copies, waits for them, and re-layouts, body(): padded.reshape(-1, points)  8.44 us
    ppermute x2, starting transfers between devices, from_behind(): lax.ppermute(value, axis, [(source, source + steps) for source in range(l...  6.96 us
  transfers between devices with their start and end apart: 5, of which 4 were waited for; matrix products, arithmetic and copies ran while one was open for 3% of the time, Pallas kernels for 0%

commit v1 on v0

--- a/solution.py
+++ b/solution.py
@@ -96,7 +96,12 @@
     local_spec = jnp.einsum(
         "xbtvp,tkr->kbrxvp", smoothed, dft_table(), precision=lax.Precision.HIGHEST
     ).astype(jnp.bfloat16)
-    spectra = lax.all_to_all(local_spec, "freq", split_axis=0, concat_axis=1, tiled=True)
+    spectra = jnp.concatenate(
+        lax.all_to_all(
+            jnp.stack(jnp.split(local_spec, lax.axis_size("freq"), axis=0)), "freq", 0, 0
+        ),
+        axis=1,
+    )
     freq_count = spectra.shape[0]
     columns = 2 * spectra.shape[1]
     values = spectra.astype(jnp.float32).reshape(

time: 304 us -> 306 us (level)
  no operation moved by 1% of the time
where the time goes in v1:
time: 306 us
  waiting for transfers between devices  165 us (54%)
  other arithmetic  39.7 us (13%)
  blocking collectives  31.8 us (10%)
  matrix products  27.9 us (9%)
  local copies, waits for them, and re-layouts  22.2 us (7%)
  starting transfers between devices  17.6 us (6%)
    ppermute x2, waiting for transfers between devices, from_behind(): lax.ppermute(value, axis, [(source, source + steps) for source in range(l...  104 us
    ppermute x1, waiting for transfers between devices, padded_2(): lax.ppermute(lax.slice_in_dim(block, block.shape[dim] - width, None, axis...  50.9 us
    all_gather x1, blocking collectives, body(): lax.all_gather(local_factor.astype(jnp.bfloat16), 'slab', axis=0, tiled=T...  31.8 us
    another operation x7, other arithmetic, upper_factor(): return jnp.swapaxes(jnp.linalg.cholesky(gram), 1, 2)  23.8 us
    dot_general x3, matrix products, record_terms(): jnp.einsum('cq,cbtvp->qbtvp', select, scaled, precision=lax.Precision.HIG...  19.4 us
    all_to_all x1, waiting for transfers between devices, body(): lax.all_to_all(jnp.stack(jnp.split(local_spec, lax.axis_size('freq'), axi...  9.9 us
    reshape x1, local copies, waits for them, and re-layouts, body(): padded.reshape(-1, points)  8.44 us
    ppermute x2, starting transfers between devices, from_behind(): lax.ppermute(value, axis, [(source, source + steps) for source in range(l...  6.96 us
  transfers between devices with their start and end apart: 5, of which 4 were waited for; matrix products, arithmetic and copies ran while one was open for 3% of the time, Pallas kernels for 0%

profile of v1, /device:TPU:0, one launch (start us, length us, event | category | flops | bytes accessed | tf_op | source)
XLA Modules:
  0.0 305.5 jit_solution(17202280778373783434)
XLA Ops:
  1.3 1.4 fusion.54
  4.5 3.2 %convert_multiply_fusion.2 = (f32[2,8,32,5,256]{4,2,3,1,0:T(8,128)S(1)}, f32[2,8,32,5,256]{4,2,3,1,0:T(8,128)S(1)}, f32[2,8,32,5,256]{4,2,3,1,0:T(8,128)S(1)}) fusion(f32[2,256]{1,0:T(2,128)S(1)} %get-tuple-element.21, bf16[1,3,2,8,32,5,256]{6,4,5,3,2,1,0:T(8,128)(2,1)} %param.6, f32[2,256]{1,0:T(2,128)S(1)} %get-tuple-element.22, ...), kind=kLoop, calls=%fused_computation.12 | loop fusion | flops 3932160 | bytes 11802624 | tf_op jit(solution)/shard_map/mul | solution.py:59
  7.7 5.8 %fusion.9 = f32[2,8,32,5,256]{4,0,3,2,1:T(2,128)S(1)} fusion(f32[2,8,32,5,256]{4,2,3,1,0:T(8,128)S(1)} %get-tuple-element.16, pred[2]{0:T(512)(128)(4,1)S(1)} %iota_compare_fusion.3, s32[2]{0:T(128)S(1)} %get-tuple-element.13), kind=kOutput, calls=%fused_computation.19 | convolution fusion | flops 15728648 | bytes 5242890 | tf_op jit(solution)/shard_map/cq,cbtvp->qbtvp/dot_general | solution.py:60
  15.5 5.8 %fusion.7 = f32[2,8,32,5,256]{4,0,3,2,1:T(2,128)S(1)} fusion(f32[2,8,32,5,256]{4,2,3,1,0:T(8,128)S(1)} %get-tuple-element.15, pred[2]{0:T(512)(128)(4,1)S(1)} %iota_compare_fusion.2, s32[2]{0:T(128)S(1)} %get-tuple-element.12), kind=kOutput, calls=%fused_computation.17 | convolution fusion | flops 15728648 | bytes 5242890 | tf_op jit(solution)/shard_map/cq,cbtvp->qbtvp/dot_general | solution.py:60
  21.4 5.7 %collective-permute-start.1 = (f32[2,8,32,5,256]{4,0,3,2,1:T(2,128)S(1)}, f32[2,8,32,5,256]{4,0,3,2,1:T(2,128)S(1)}, u32[]{:S(2)}, u32[]{:S(2)}) collective-permute-start(f32[2,8,32,5,256]{4,0,3,2,1:T(2,128)S(1)} %fusion.7), channel_id=1, source_target_pairs={{0,4},{4,8},{8,12},{12,16},{16,20},{20,24},{24,28},{1,5},{5,9},{9,... | collective-permute-start | bytes 7864328 | tf_op jit(solution)/shard_map/ppermute | solution.py:17
  27.7 47.6 %collective-permute-done = f32[2,8,32,5,256]{4,0,3,2,1:T(2,128)S(1)} collective-permute-done((f32[2,8,32,5,256]{4,0,3,2,1:T(2,128)S(1)}, f32[2,8,32,5,256]{4,0,3,2,1:T(2,128)S(1)}, u32[]{:S(2)}, u32[]{:S(2)}) %collective-permute-start) | collective-permute-done | bytes 2621472 | tf_op jit(solution)/shard_map/ppermute | solution.py:17
  75.3 56.3 %collective-permute-done.1 = f32[2,8,32,5,256]{4,0,3,2,1:T(2,128)S(1)} collective-permute-done((f32[2,8,32,5,256]{4,0,3,2,1:T(2,128)S(1)}, f32[2,8,32,5,256]{4,0,3,2,1:T(2,128)S(1)}, u32[]{:S(2)}, u32[]{:S(2)}) %collective-permute-start.1) | collective-permute-done | bytes 2621472 | tf_op jit(solution)/shard_map/ppermute | solution.py:17
  131.6 7.8 %add_convert_fusion = bf16[2,8,32,5,256]{4,0,3,2,1:T(2,128)(2,1)S(1)} fusion(f32[2,8,32,5,256]{4,0,3,2,1:T(2,128)S(1)} %collective-permute-done.1, f32[2,8,32,5,256]{4,0,3,2,1:T(2,128)S(1)} %collective-permute-done, f32[2,8,32,5,256]{4,2,3,1,0:T(8,128)S(1)} %get-tuple-element.14, pred[2]{0:T(512)(128)(4,1)S(1)} %iota_compare_fusion.4, ...), kind=kOutput, calls=%fused_computation.16 | convolution fusion | flops 17694728 | bytes 9175050 | tf_op jit(solution)/shard_map/cq,cbtvp->qbtvp/dot_general | solution.py:60
  139.4 5.5 %collective-permute-start.2 = (bf16[2,8,32,5,256]{4,0,3,2,1:T(2,128)(2,1)S(1)}, bf16[2,8,32,5,256]{4,0,3,2,1:T(2,128)(2,1)}, u32[]{:S(2)}, u32[]{:S(2)}) collective-permute-start(bf16[2,8,32,5,256]{4,0,3,2,1:T(2,128)(2,1)S(1)} %add_convert_fusion), channel_id=1, source_target_pairs={{0,4},{4,8},{8,12},{12,16},{16,20},{20,24},{24,28},{1,5},{5,9},{9,... | collective-permute-start | bytes 3932168 | tf_op jit(solution)/shard_map/ppermute | solution.py:25
  144.9 1.5 collective-permute-start.3
  149.2 50.9 %collective-permute-done.2 = bf16[2,8,32,5,256]{4,0,3,2,1:T(2,128)(2,1)} collective-permute-done((bf16[2,8,32,5,256]{4,0,3,2,1:T(2,128)(2,1)S(1)}, bf16[2,8,32,5,256]{4,0,3,2,1:T(2,128)(2,1)}, u32[]{:S(2)}, u32[]{:S(2)}) %collective-permute-start.2) | collective-permute-done | bytes 1310752 | tf_op jit(solution)/shard_map/ppermute | solution.py:25
  200.1 5.7 %pad_maximum_fusion = bf16[6,8,32,5,256]{4,0,3,2,1:T(8,128)(2,1)S(1)} fusion(bf16[2,8,32,5,256]{4,0,3,2,1:T(2,128)(2,1)} %collective-permute-done.3, bf16[2,8,32,5,256]{4,0,3,2,1:T(2,128)(2,1)S(1)} %add_convert_fusion, bf16[2,8,32,5,256]{4,0,3,2,1:T(2,128)(2,1)} %collective-permute-done.2), kind=kLoop, calls=%fused_computation | loop fusion | flops 11796480 | bytes 7864320 | tf_op jit(solution)/shard_map/concatenate | solution.py:29
  205.8 4.1 %copy.45 = bf16[6,8,32,5,256]{4,3,2,1,0:T(8,128)(2,1)} copy(bf16[6,8,32,5,256]{4,0,3,2,1:T(8,128)(2,1)S(1)} %pad_maximum_fusion) | data formatting | bytes 7864320 | tf_op jit(solution)/shard_map/concatenate | solution.py:29
  210.0 8.4 %reshape.317 = bf16[7680,256]{1,0:T(8,128)(2,1)} reshape(bf16[6,8,32,5,256]{4,3,2,1,0:T(8,128)(2,1)} %copy.45) | data formatting | bytes 7864320 | tf_op jit(solution)/shard_map/reshape | solution.py:90
  218.4 3.3 %fusion.55 = f32[7680,256]{1,0:T(8,128)S(1)} fusion(bf16[7680,256]{1,0:T(8,128)(2,1)} %reshape.317, bf16[256,256]{1,0:T(8,128)(2,1)S(1)} %convert_element_type.143), kind=kOutput, calls=%fused_computation.98 | convolution fusion | flops 1006632960 | bytes 11927552 | tf_op jit(solution)/shard_map/dot_general | solution.py:90
  222.5 2.1 reshape.327
  224.7 4.2 %fusion.21 = bf16[8,8,2,2,5,256]{5,0,4,1,3,2:T(8,128)(2,1)S(1)} fusion(f32[2,8,32,5,256]{4,3,2,1,0:T(8,128)} %reshape.327, f32[32,8,1]{0,1,2:T(8,128)S(1)} %get-tuple-element.25, f32[32,8,1]{0,1,2:T(8,128)S(1)} %get-tuple-element.24), kind=kOutput, calls=%fused_computation.28 | convolution fusion | flops 126157312 | bytes 3278848 | tf_op jit(solution)/shard_map/xbtvp,tkr->kbrxvp/dot_general | solution.py:96
  229.4 2.1 pad_maximum_fusion.1
  231.5 3.7 %all-to-all-start = ((bf16[4,2,8,2,2,5,256]{6,1,5,2,4,3,0:T(2,128)(2,1)}), bf16[4,2,8,2,2,5,256]{6,1,5,2,4,3,0:T(2,128)(2,1)S(1)}, u32[]{:S(2)}, u32[]{:S(2)}) async-start(bf16[4,2,8,2,2,5,256]{6,1,5,2,4,3,0:T(2,128)(2,1)} %pad_maximum_fusion.1), calls=%async_computation | async-start | bytes 1310720 | tf_op jit(solution)/shard_map/all_to_all | solution.py:100
  235.2 9.9 %all-to-all-done = bf16[4,2,8,2,2,5,256]{6,1,5,2,4,3,0:T(2,128)(2,1)S(1)} async-done(((bf16[4,2,8,2,2,5,256]{6,1,5,2,4,3,0:T(2,128)(2,1)}), bf16[4,2,8,2,2,5,256]{6,1,5,2,4,3,0:T(2,128)(2,1)S(1)}, u32[]{:S(2)}, u32[]{:S(2)}) %all-to-all-start) | async-done | bytes 655392 | tf_op jit(solution)/shard_map/all_to_all | solution.py:100
  247.1 11.7 %custom-call.4 = f32[2,64,64]{2,1,0:T(8,128)S(1)} custom-call(f32[2,64,64]{2,1,0:T(8,128)S(1)} %fusion.26), custom_call_target="Cholesky" | custom-call | tf_op jit(solution)/shard_map/jit(cholesky)/cholesky | solution.py:64
  259.2 31.8 %all-gather = bf16[16,64,64]{2,1,0:T(8,128)(2,1)S(1)} all-gather(bf16[2,64,64]{2,1,0:T(8,128)(2,1)S(1)} %copy.50), channel_id=2, replica_groups=mesh['slab'=8,'freq'=4] {'slab'}, dimensions={0}, use_global_device_ids=true | all-gather | bytes 147456 | tf_op jit(solution)/shard_map/all_gather | solution.py:117
  291.3 11.7 %custom-call.5 = f32[2,64,64]{2,1,0:T(8,128)S(1)} custom-call(f32[2,64,64]{2,1,0:T(8,128)S(1)} %fusion.25), custom_call_target="Cholesky" | custom-call | tf_op jit(solution)/shard_map/jit(cholesky)/cholesky | solution.py:64
  304.0 1.5 copy.53
  (40 shorter events, 12.0 us)
Async XLA Ops:
  13.6 61.7 %collective-permute-start = (f32[2,8,32,5,256]{4,0,3,2,1:T(2,128)S(1)}, f32[2,8,32,5,256]{4,0,3,2,1:T(2,128)S(1)}, u32[]{:S(2)}, u32[]{:S(2)}) collective-permute-start(f32[2,8,32,5,256]{4,0,3,2,1:T(2,128)S(1)} %fusion.9), channel_id=1, source_target_pairs={{4,0},{8,4},{12,8},{16,12},{20,16},{24,20},{28,24},{5,1},{9,5},{13... | collective-permute-start | bytes 7864328 | tf_op jit(solution)/shard_map/ppermute | solution.py:17
  21.4 110.3 %collective-permute-start.1 = (f32[2,8,32,5,256]{4,0,3,2,1:T(2,128)S(1)}, f32[2,8,32,5,256]{4,0,3,2,1:T(2,128)S(1)}, u32[]{:S(2)}, u32[]{:S(2)}) collective-permute-start(f32[2,8,32,5,256]{4,0,3,2,1:T(2,128)S(1)} %fusion.7), channel_id=1, source_target_pairs={{0,4},{4,8},{8,12},{12,16},{16,20},{20,24},{24,28},{1,5},{5,9},{9,... | collective-permute-start | bytes 7864328 | tf_op jit(solution)/shard_map/ppermute | solution.py:17
  139.4 60.7 %collective-permute-start.2 = (bf16[2,8,32,5,256]{4,0,3,2,1:T(2,128)(2,1)S(1)}, bf16[2,8,32,5,256]{4,0,3,2,1:T(2,128)(2,1)}, u32[]{:S(2)}, u32[]{:S(2)}) collective-permute-start(bf16[2,8,32,5,256]{4,0,3,2,1:T(2,128)(2,1)S(1)} %add_convert_fusion), channel_id=1, source_target_pairs={{0,4},{4,8},{8,12},{12,16},{16,20},{20,24},{24,28},{1,5},{5,9},{9,... | collective-permute-start | bytes 3932168 | tf_op jit(solution)/shard_map/ppermute | solution.py:25
  144.9 55.2 %collective-permute-start.3 = (bf16[2,8,32,5,256]{4,0,3,2,1:T(2,128)(2,1)S(1)}, bf16[2,8,32,5,256]{4,0,3,2,1:T(2,128)(2,1)}, u32[]{:S(2)}, u32[]{:S(2)}) collective-permute-start(bf16[2,8,32,5,256]{4,0,3,2,1:T(2,128)(2,1)S(1)} %add_convert_fusion), channel_id=1, source_target_pairs={{4,0},{8,4},{12,8},{16,12},{20,16},{24,20},{28,24},{5,1},{9,5},{13... | collective-permute-start | bytes 3932168 | tf_op jit(solution)/shard_map/ppermute | solution.py:28
  228.9 6.3 %copy-start = (f32[2,256]{1,0:T(2,128)S(1)}, f32[2,256]{1,0:T(2,128)}, u32[]{:S(2)}) copy-start(f32[2,256]{1,0:T(2,128)} %param.10) | copy-start | bytes 6148
  231.5 13.7 %all-to-all-start = ((bf16[4,2,8,2,2,5,256]{6,1,5,2,4,3,0:T(2,128)(2,1)}), bf16[4,2,8,2,2,5,256]{6,1,5,2,4,3,0:T(2,128)(2,1)S(1)}, u32[]{:S(2)}, u32[]{:S(2)}) async-start(bf16[4,2,8,2,2,5,256]{6,1,5,2,4,3,0:T(2,128)(2,1)} %pad_maximum_fusion.1), calls=%async_computation | async-start | bytes 1310720 | tf_op jit(solution)/shard_map/all_to_all | solution.py:100
